TPU v7x, 512 devices: a whole 4x8x8 slice. The times are simulated.
512 devices in a mesh: centre: 16 (over y, core), sample: 32 (over z, x).
Axes of the slice: x: 4, y: 8, z: 8, core: 2. Of those that a mesh axis runs over, the one named last changes fastest.
Arguments:
- centres: bfloat16 [1024, 32768], P(None, 'centre'), may hold values from -40 to 40
- pool: bfloat16 [1024, 32768], P('centre', 'sample'), may hold values from -40 to 40
- labels: int32 [32768], P('sample'), may hold values from 0 to 143
- picks: int32 [2, 16384], P(None, 'sample'), may hold values from 0 to 32767, as said below
- coefs: float32 [144, 32768], P(None, ('centre', 'sample')), may hold values from -192 to 1024000
Outputs:
- new_coefs: float32 [144, 32768], P(None, ('centre', 'sample'))
Inputs may be any that keep to these rules, and one draw needn't show every extreme that they name: `picks`: entry b of a step's batch is a pool column in [(b // 512) * 1024, (b // 512 + 1) * 1024); entries may repeat.
All inputs are finite; a program needn't handle non-finite values.
Results may differ from a plain program's by a relative error of at most 0.00065.
Values may be sent and summed in bfloat16 or wider, within the bound.
No kernel may reach another device: no remote copies, remote signals or barrier semaphores. Data moves between devices by JAX's collectives and lax.ppermute only.
A program may use at most 64 MiB of HBM per device.

v0:
```python
import jax
import jax.numpy as jnp
from jax import lax
from jax.sharding import PartitionSpec as P

STEPS = 2
LOGIT_GAIN = 16.0
LENGTH_SCALE = 0.5
STEP_GAIN = 2048.0
EPS = 1e-06


def from_everyone(array, axis):
    peers = lax.axis_size(axis)
    return lax.all_to_all(
        jnp.broadcast_to(array[None], (peers, *array.shape)), axis, 0, 0, tiled=True
    )


def joined_along(parts, dim):
    dims = list(parts.shape[1:])
    dims[dim] *= parts.shape[0]
    return jnp.moveaxis(parts, 0, dim).reshape(dims)


def collect(array, axis, dim):
    parts = from_everyone(array, axis)
    return joined_along(parts, dim)


def over_pieces(array, axis):
    return lax.all_gather(array, axis).sum(0)


def cut_along(array, dim, peers):
    dims = array.shape
    parts = array.reshape(*dims[:dim], peers, dims[dim] // peers, *dims[dim + 1 :])
    return jnp.moveaxis(parts, dim, 0)


def summed_on_arrival(array, axis, dim):
    peers = lax.axis_size(axis)
    parts = lax.all_to_all(cut_along(array, dim, peers), axis, 0, 0, tiled=True)
    return jnp.sum(parts, axis=0)


def laplace(cross, sample_sq, centre_sq, width):
    mean_sq = (sample_sq[:, None] + centre_sq[None, :] - 2.0 * cross) / width
    return jnp.exp(-jnp.sqrt(mean_sq + EPS) / LENGTH_SCALE).astype(jnp.bfloat16)


def on_device(centres, pool, labels, picks, coefs):
    width = centres.shape[0]
    cen_dev = centres.shape[1]
    pool_dev = pool.shape[1]
    batch_dev = picks.shape[1]
    classes = coefs.shape[0]
    total_centres = cen_dev * lax.axis_size("centre")
    total_batch = batch_dev * lax.axis_size("sample")
    rate = STEP_GAIN * LOGIT_GAIN / total_batch
    centre_sq = jnp.sum(jnp.square(centres.astype(jnp.float32)), axis=0)
    local_picks = picks - lax.axis_index("sample") * pool_dev
    current = coefs
    for step in range(STEPS):
        coef_half = collect(current.astype(jnp.bfloat16), "sample", 1)
        chosen = local_picks[step]
        feats = jnp.take(pool, chosen, axis=1)
        labs = jnp.take(labels, chosen)
        gathered = lax.all_gather(feats, "centre", axis=0, tiled=True)
        cross = lax.dot_general(
            gathered, centres, (((0,), (0,)), ((), ())), preferred_element_type=jnp.float32
        )
        sample_sq = jnp.sum(jnp.square(gathered.astype(jnp.float32)), axis=0)
        kern = laplace(cross, sample_sq, centre_sq, width)
        partial_logits = lax.dot_general(
            coef_half, kern, (((1,), (1,)), ((), ())), preferred_element_type=jnp.float32
        )
        logits = over_pieces(partial_logits, "centre") * (LOGIT_GAIN / total_centres)
        top = jnp.max(logits, axis=0, keepdims=True)
        expo = jnp.exp(logits - top)
        probs = expo / jnp.sum(expo, axis=0, keepdims=True)
        class_ids = jnp.arange(classes, dtype=jnp.int32)
        onehot = (class_ids[:, None] == labs[None, :]).astype(jnp.float32)
        resid = (probs - onehot).astype(jnp.bfloat16)
        grad_part = jnp.dot(resid, kern, preferred_element_type=jnp.float32)
        current = current - rate * summed_on_arrival(grad_part, "sample", 1)
    return current


def solution(mesh):
    placed = (
        P(None, "centre"),
        P("centre", "sample"),
        P("sample"),
        P(None, "sample"),
        P(None, ("centre", "sample")),
    )
    return jax.shard_map(
        on_device,
        mesh=mesh,
        in_specs=placed,
        out_specs=P(None, ("centre", "sample")),
        check_vma=False,
    )
```

profile of v0, /device:TPU:2, one launch (start us, length us, event | category | flops | bytes accessed | tf_op | source)
XLA Modules:
  0.0 336.5 jit_solution(12417494301291164431)
XLA Ops:
  6.5 0.7 broadcast_subtract_fusion
  7.3 2.3 gather_fusion.1
  9.6 1.1 copy.40
  10.7 1.3 gather_fusion
  12.0 0.1 select_bitcast_fusion.1
  12.2 0.7 copy.41
  12.9 0.0 all-gather.7.cloned.1.call-update
  12.9 0.8 convert_element_type.36
  13.8 1.2 broadcast_in_dim.19
  14.9 13.5 %all-to-all-start = ((bf16[32,144,64]{1,2,0:T(8,128)(2,1)}), bf16[32,144,64]{1,2,0:T(8,128)(2,1)S(1)}, u32[]{:S(2)}, u32[]{:S(2)}) async-start(bf16[32,144,64]{1,2,0:T(8,128)(2,1)} %broadcast_in_dim.19), calls=%async_computation | async-start | bytes 2097152 | tf_op jit(solution)/shard_map/all_to_all | solution.py:15
  28.4 0.0 all-gather.11.cloned.1.call-start
  28.4 3.1 multiply_reduce_fusion
  31.5 27.1 %all-gather.7.cloned.1.call-done = bf16[1024,512]{1,0:T(8,128)(2,1)} async-done(((bf16[64,512]{1,0:T(8,128)(2,1)}), bf16[1024,512]{1,0:T(8,128)(2,1)}) %all-gather.7.cloned.1.call-update) | async-done | bytes 1048592 | tf_op jit(solution)/shard_map/all_gather | solution.py:69
  58.6 1.5 multiply_reduce_fusion.2
  60.1 6.8 %exponential_convert_fusion.1 = bf16[512,2048]{1,0:T(8,128)(2,1)S(1)} fusion(bf16[1024,512]{1,0:T(8,128)(2,1)} %all-gather.7.cloned.1.call-done, bf16[1024,2048]{1,0:T(8,128)(2,1)} %param.9, f32[2048]{0:T(1024)S(1)} %multiply_reduce_fusion, f32[512]{0:T(512)S(1)} %multiply_reduce_fusion.2), kind=kOutput, calls=%fused_computation.6 | convolution fusion | flops 2155872256 | bytes 7350272 | tf_op jit(solution)/shard_map/dot_general | solution.py:70
  66.9 1.6 convolution_bitcast_fusion
  68.4 0.0 all-gather.11.cloned.1.call-update
  68.4 44.5 %all-gather.11.cloned.1.call-done = f32[2304,512]{1,0:T(8,128)} async-done(((f32[144,512]{1,0:T(8,128)}), f32[2304,512]{1,0:T(8,128)}) %all-gather.11.cloned.1.call-update) | async-done | bytes 4718608 | tf_op jit(solution)/shard_map/all_gather | solution.py:32
  113.0 2.9 reduce_sum.83
  115.9 0.1 fusion
  116.0 1.6 fusion.2
  117.5 2.1 reshape.34
  119.6 2.4 copy.43
  122.0 10.6 %all-to-all-start.1 = ((f32[32,144,64]{1,2,0:T(8,128)}), f32[32,144,64]{1,2,0:T(8,128)S(1)}, u32[]{:S(2)}, u32[]{:S(2)}) async-start(f32[32,144,64]{1,2,0:T(8,128)} %copy.43), calls=%async_computation.1 | async-start | bytes 4194304 | tf_op jit(solution)/shard_map/all_to_all | solution.py:43
  132.7 0.0 all-gather.9.cloned.1.call-start
  132.7 2.3 gather_fusion.3
  135.0 1.3 gather_fusion.2
  136.4 0.1 select_bitcast_fusion
  136.6 0.7 copy.48
  137.3 45.0 %all-to-all-done.1 = f32[32,144,64]{1,2,0:T(8,128)S(1)} async-done(((f32[32,144,64]{1,2,0:T(8,128)}), f32[32,144,64]{1,2,0:T(8,128)S(1)}, u32[]{:S(2)}, u32[]{:S(2)}) %all-to-all-start.1) | async-done | bytes 1179680 | tf_op jit(solution)/shard_map/all_to_all | solution.py:43
  182.3 0.1 reduce_sum.85
  182.5 1.1 broadcast_in_dim.20
  183.6 6.5 %all-to-all-start.2 = ((bf16[32,144,64]{1,2,0:T(8,128)(2,1)}), bf16[32,144,64]{1,2,0:T(8,128)(2,1)S(1)}, u32[]{:S(2)}, u32[]{:S(2)}) async-start(bf16[32,144,64]{1,2,0:T(8,128)(2,1)} %broadcast_in_dim.20), calls=%async_computation.2 | async-start | bytes 2097152 | tf_op jit(solution)/shard_map/all_to_all | solution.py:15
  190.1 0.0 all-gather.13.cloned.1.call-start
  190.1 0.0 all-gather.9.cloned.1.call-done
  190.2 1.5 multiply_reduce_fusion.1
  191.7 6.7 %exponential_convert_fusion = bf16[512,2048]{1,0:T(8,128)(2,1)S(1)} fusion(bf16[1024,512]{1,0:T(8,128)(2,1)} %all-gather.9.cloned.1.call-done, bf16[1024,2048]{1,0:T(8,128)(2,1)} %param.9, f32[512]{0:T(512)S(1)} %multiply_reduce_fusion.1, f32[2048]{0:T(1024)S(1)} %multiply_reduce_fusion), kind=kOutput, calls=%fused_computation.5 | convolution fusion | flops 2155872256 | bytes 7350272 | tf_op jit(solution)/shard_map/dot_general | solution.py:70
  198.4 19.8 %all-to-all-done.2 = bf16[32,144,64]{1,2,0:T(8,128)(2,1)S(1)} async-done(((bf16[32,144,64]{1,2,0:T(8,128)(2,1)}), bf16[32,144,64]{1,2,0:T(8,128)(2,1)S(1)}, u32[]{:S(2)}, u32[]{:S(2)}) %all-to-all-start.2) | async-done | bytes 589856 | tf_op jit(solution)/shard_map/all_to_all | solution.py:15
  218.2 1.6 fusion.16
  219.8 39.4 %all-gather.13.cloned.1.call-done = f32[2304,512]{1,0:T(8,128)} async-done(((f32[144,512]{1,0:T(8,128)}), f32[2304,512]{1,0:T(8,128)}) %all-gather.13.cloned.1.call-update) | async-done | bytes 4718608 | tf_op jit(solution)/shard_map/all_gather | solution.py:32
  259.2 2.9 reduce_sum.87
  262.1 0.1 fusion.1
  262.1 2.1 fusion.3
  264.3 0.9 reshape.36
  265.2 2.4 copy.49
  267.6 61.6 %all_to_all.20 = f32[32,144,64]{1,2,0:T(8,128)S(1)} all-to-all(f32[32,144,64]{1,2,0:T(8,128)} %copy.49), channel_id=1, replica_groups=mesh['centre'=16,'sample'=32] {'sample'}, dimensions={0} | all-to-all | bytes 2359296 | tf_op jit(solution)/shard_map/all_to_all | solution.py:43
  329.2 0.1 reduce_sum.89
  329.4 0.6 multiply_subtract_fusion
  (26 shorter events, 0.2 us)
Async XLA Ops:
  6.5 0.7 copy-start
  6.5 52.0 %all-gather.7.cloned.1.call-start = ((), (), s32[]{:S(2)}) async-start(), calls=%async_computation.4 | async-start | bytes 1114112 | tf_op jit(solution)/shard_map/all_gather | solution.py:69
  14.9 51.9 %all-to-all-start = ((bf16[32,144,64]{1,2,0:T(8,128)(2,1)}), bf16[32,144,64]{1,2,0:T(8,128)(2,1)S(1)}, u32[]{:S(2)}, u32[]{:S(2)}) async-start(bf16[32,144,64]{1,2,0:T(8,128)(2,1)} %broadcast_in_dim.19), calls=%async_computation | async-start | bytes 2097152 | tf_op jit(solution)/shard_map/all_to_all | solution.py:15
  28.4 84.6 %all-gather.11.cloned.1.call-start = ((), (), s32[]{:S(2)}) async-start(), calls=%async_computation.6 | async-start | bytes 5013504 | tf_op jit(solution)/shard_map/all_gather | solution.py:32
  122.0 60.4 %copy-start.4 = (f32[144,64]{0,1:T(8,128)S(1)}, f32[144,64]{0,1:T(8,128)}, u32[]{:S(2)}) copy-start(f32[144,64]{0,1:T(8,128)} %param.13) | copy-start | bytes 110596
  122.0 60.3 %all-to-all-start.1 = ((f32[32,144,64]{1,2,0:T(8,128)}), f32[32,144,64]{1,2,0:T(8,128)S(1)}, u32[]{:S(2)}, u32[]{:S(2)}) async-start(f32[32,144,64]{1,2,0:T(8,128)} %copy.43), calls=%async_computation.1 | async-start | bytes 4194304 | tf_op jit(solution)/shard_map/all_to_all | solution.py:43
  132.7 57.5 %all-gather.9.cloned.1.call-start = ((), (), s32[]{:S(2)}) async-start(), calls=%async_computation.5 | async-start | bytes 1114112 | tf_op jit(solution)/shard_map/all_gather | solution.py:69
  182.5 7.7 %copy-start.2 = (f32[144,64]{0,1:T(8,128)}, f32[144,64]{0,1:T(8,128)S(1)}, u32[]{:S(2)}) copy-start(f32[144,64]{0,1:T(8,128)S(1)} %reduce_sum.85) | copy-start | bytes 110596
  183.6 34.6 %all-to-all-start.2 = ((bf16[32,144,64]{1,2,0:T(8,128)(2,1)}), bf16[32,144,64]{1,2,0:T(8,128)(2,1)S(1)}, u32[]{:S(2)}, u32[]{:S(2)}) async-start(bf16[32,144,64]{1,2,0:T(8,128)(2,1)} %broadcast_in_dim.20), calls=%async_computation.2 | async-start | bytes 2097152 | tf_op jit(solution)/shard_map/all_to_all | solution.py:15
  190.1 69.1 %all-gather.13.cloned.1.call-start = ((), (), s32[]{:S(2)}) async-start(), calls=%async_computation.7 | async-start | bytes 5013504 | tf_op jit(solution)/shard_map/all_gather | solution.py:32
  198.4 60.7 %copy-start.1 = (bf16[512,2048]{1,0:T(8,128)(2,1)}, bf16[512,2048]{1,0:T(8,128)(2,1)S(1)}, u32[]{:S(2)}) copy-start(bf16[512,2048]{1,0:T(8,128)(2,1)S(1)} %exponential_convert_fusion) | copy-start | bytes 6291460
  267.6 61.7 %copy-start.3 = (f32[144,64]{0,1:T(8,128)S(1)}, f32[144,64]{0,1:T(8,128)}, u32[]{:S(2)}) copy-start(f32[144,64]{0,1:T(8,128)} %copy-done.2) | copy-start | bytes 110596
  267.6 61.7 %copy-start.5 = (f32[144,64]{0,1:T(8,128)S(1)}, f32[144,64]{0,1:T(8,128)}, u32[]{:S(2)}) copy-start(f32[144,64]{0,1:T(8,128)} %param.13) | copy-start | bytes 110596
Sparse Core Ops, SparseCore 0:
  13.0 45.5 all-gather.6
  68.6 44.3 all-gather.10
  137.4 38.9 all-gather.8
  219.9 39.2 all-gather.12
where the time goes:
time: 337 us
  waiting for transfers between devices  176 us (52%)
  blocking collectives  61.6 us (18%)
  starting transfers between devices  30.7 us (9%)
  matrix products  20.3 us (6%)
  local copies, waits for them, and re-layouts  19.9 us (6%)
  other arithmetic  14.8 us (4%)
  between operations  13.4 us (4%)
    all_gather x2, waiting for transfers between devices, over_pieces(): return lax.all_gather(array, axis).sum(0)  83.9 us
    all_to_all x1, blocking collectives, summed_on_arrival(): parts = lax.all_to_all(cut_along(array, dim, peers), axis, 0, 0, tiled=True)  61.6 us
    all_to_all x1, waiting for transfers between devices, summed_on_arrival(): parts = lax.all_to_all(cut_along(array, dim, peers), axis, 0, 0, tiled=True)  45 us
    all_gather x2, waiting for transfers between devices, on_device(): gathered = lax.all_gather(feats, 'centre', axis=0, tiled=True)  27.1 us
    all_to_all x2, starting transfers between devices, from_everyone(): lax.all_to_all(jnp.broadcast_to(array[None], (peers, *array.shape)), axis...  19.9 us
    all_to_all x2, waiting for transfers between devices, from_everyone(): lax.all_to_all(jnp.broadcast_to(array[None], (peers, *array.shape)), axis...  19.8 us
    dot_general x2, matrix products, on_device(): lax.dot_general(gathered, centres, (((0,), (0,)), ((), ())), preferred_el...  13.5 us
    all_to_all x1, starting transfers between devices, summed_on_arrival(): parts = lax.all_to_all(cut_along(array, dim, peers), axis, 0, 0, tiled=True)  10.6 us
  transfers between devices with their start and end apart: 7, of which 5 were waited for; matrix products, arithmetic and copies ran while one was open for 8% of the time, Pallas kernels for 0%

commit v1 on v0

--- a/solution.py
+++ b/solution.py
@@ -66,7 +66,9 @@
         chosen = local_picks[step]
         feats = jnp.take(pool, chosen, axis=1)
         labs = jnp.take(labels, chosen)
-        gathered = lax.all_gather(feats, "centre", axis=0, tiled=True)
+        gathered = jnp.concatenate(
+            lax.all_to_all(jnp.stack([feats] * lax.axis_size("centre")), "centre", 0, 0), axis=0
+        )
         cross = lax.dot_general(
             gathered, centres, (((0,), (0,)), ((), ())), preferred_element_type=jnp.float32
         )

time: 337 us -> 392 us (1.16)
  waiting for transfers between devices: 176 us -> 221 us
  starting transfers between devices: 30.7 us -> 42.1 us
    all_to_all x0 -> x2, waiting for transfers between devices: none -> 53.1 us  [on_device(): lax.all_to_all(jnp.stack([feats] * lax.axis_size('centre')), 'centre', 0, 0)]
    all_gather x2 -> x0, waiting for transfers between devices: 27.1 us -> none  [on_device(): gathered = lax.all_gather(feats, 'centre', axis=0, tiled=True)]
    all_to_all x2, waiting for transfers between devices: 19.8 us -> 42.9 us  [from_everyone(): lax.all_to_all(jnp.broadcast_to(array[None], (peers, *array.shape)), axis...]
    all_to_all x0 -> x2, starting transfers between devices: none -> 11.5 us  [on_device(): lax.all_to_all(jnp.stack([feats] * lax.axis_size('centre')), 'centre', 0, 0)]
    all_gather x2, waiting for transfers between devices: 83.9 us -> 78.9 us  [over_pieces(): return lax.all_gather(array, axis).sum(0)]
  transfers between devices with their start and end apart: 7 -> 7, of which waited for: 5 -> 7; matrix products, arithmetic and copies ran while one was open for 8% -> 5% of each run, Pallas kernels for 0% -> 0%
where the time goes in v1:
time: 392 us; the launch traced here: 391 us
  waiting for transfers between devices  221 us (56%)
  blocking collectives  61.6 us (16%)
  starting transfers between devices  42.1 us (11%)
  local copies, waits for them, and re-layouts  20.9 us (5%)
  matrix products  20 us (5%)
  between operations  13.7 us (3%)
  other arithmetic  11.7 us (3%)
    all_gather x2, waiting for transfers between devices, over_pieces(): return lax.all_gather(array, axis).sum(0)  78.9 us
    all_to_all x1, blocking collectives, summed_on_arrival(): parts = lax.all_to_all(cut_along(array, dim, peers), axis, 0, 0, tiled=True)  61.6 us
    all_to_all x2, waiting for transfers between devices, on_device(): lax.all_to_all(jnp.stack([feats] * lax.axis_size('centre')), 'centre', 0, 0)  53.1 us
    all_to_all x1, waiting for transfers between devices, summed_on_arrival(): parts = lax.all_to_all(cut_along(array, dim, peers), axis, 0, 0, tiled=True)  45.6 us
    all_to_all x2, waiting for transfers between devices, from_everyone(): lax.all_to_all(jnp.broadcast_to(array[None], (peers, *array.shape)), axis...  42.9 us
    all_to_all x2, starting transfers between devices, from_everyone(): lax.all_to_all(jnp.broadcast_to(array[None], (peers, *array.shape)), axis...  19.9 us
    all_to_all x2, starting transfers between devices, on_device(): lax.all_to_all(jnp.stack([feats] * lax.axis_size('centre')), 'centre', 0, 0)  11.5 us
    dot_general x2, matrix products, on_device(): lax.dot_general(gathered, centres, (((0,), (0,)), ((), ())), preferred_el...  10.7 us
  transfers between devices with their start and end apart: 7, of which 7 were waited for; matrix products, arithmetic and copies ran while one was open for 5% of the time, Pallas kernels for 0%

profile of v1, /device:TPU:2, one launch (start us, length us, event | category | flops | bytes accessed | tf_op | source)
XLA Modules:
  0.0 390.6 jit_solution(17241617665069122735)
XLA Ops:
  6.5 0.7 broadcast_subtract_fusion
  7.3 2.3 gather_fusion.1
  9.6 1.1 copy.44
  10.7 1.3 gather_fusion
  12.0 0.1 select_bitcast_fusion.1
  12.2 0.1 copy.45
  12.3 1.1 stack.4
  13.4 7.2 %all-to-all-start = ((bf16[16,64,512]{2,1,0:T(8,128)(2,1)}), bf16[16,64,512]{2,1,0:T(8,128)(2,1)S(1)}, u32[]{:S(2)}, u32[]{:S(2)}) async-start(bf16[16,64,512]{2,1,0:T(8,128)(2,1)} %stack.4), calls=%async_computation | async-start | bytes 2097152 | tf_op jit(solution)/shard_map/all_to_all | solution.py:70
  20.6 26.6 %all-to-all-done = bf16[16,64,512]{2,1,0:T(8,128)(2,1)S(1)} async-done(((bf16[16,64,512]{2,1,0:T(8,128)(2,1)}), bf16[16,64,512]{2,1,0:T(8,128)(2,1)S(1)}, u32[]{:S(2)}, u32[]{:S(2)}) %all-to-all-start) | async-done | bytes 1048608 | tf_op jit(solution)/shard_map/all_to_all | solution.py:70
  47.3 1.2 broadcast_in_dim.19
  48.4 13.5 %all-to-all-start.1 = ((bf16[32,144,64]{1,2,0:T(8,128)(2,1)}), bf16[32,144,64]{1,2,0:T(8,128)(2,1)}, u32[]{:S(2)}, u32[]{:S(2)}) async-start(bf16[32,144,64]{1,2,0:T(8,128)(2,1)} %broadcast_in_dim.19), calls=%async_computation.1 | async-start | bytes 2097152 | tf_op jit(solution)/shard_map/all_to_all | solution.py:15
  61.9 0.0 all-gather.5.cloned.1.call-start
  62.0 3.2 multiply_reduce_fusion
  65.2 0.3 multiply_reduce_fusion.2
  65.5 4.3 %exponential_convert_fusion.1 = bf16[512,2048]{1,0:T(8,128)(2,1)S(1)} fusion(bf16[1024,512]{1,0:T(8,128)(2,1)S(1)} %bitcast.35, bf16[1024,2048]{1,0:T(8,128)(2,1)S(1)} %copy-done.1, f32[2048]{0:T(1024)S(1)} %multiply_reduce_fusion, f32[512]{0:T(512)S(1)} %multiply_reduce_fusion.2), kind=kOutput, calls=%fused_computation.6 | convolution fusion | flops 2155872256 | bytes 7350272 | tf_op jit(solution)/shard_map/dot_general | solution.py:72
  69.8 20.9 %all-to-all-done.1 = bf16[32,144,64]{1,2,0:T(8,128)(2,1)} async-done(((bf16[32,144,64]{1,2,0:T(8,128)(2,1)}), bf16[32,144,64]{1,2,0:T(8,128)(2,1)}, u32[]{:S(2)}, u32[]{:S(2)}) %all-to-all-start.1) | async-done | bytes 589856 | tf_op jit(solution)/shard_map/all_to_all | solution.py:15
  90.7 2.8 convolution_bitcast_fusion
  93.5 39.5 %all-gather.5.cloned.1.call-done = f32[2304,512]{1,0:T(8,128)} async-done(((f32[144,512]{1,0:T(8,128)}), f32[2304,512]{1,0:T(8,128)}) %all-gather.5.cloned.1.call-update) | async-done | bytes 4718608 | tf_op jit(solution)/shard_map/all_gather | solution.py:32
  133.0 2.9 reduce_sum.83
  135.9 0.1 fusion
  136.0 1.6 fusion.2
  137.5 2.1 reshape.45
  139.6 2.4 copy.47
  142.0 10.5 %all-to-all-start.2 = ((f32[32,144,64]{1,2,0:T(8,128)}), f32[32,144,64]{1,2,0:T(8,128)S(1)}, u32[]{:S(2)}, u32[]{:S(2)}) async-start(f32[32,144,64]{1,2,0:T(8,128)} %copy.47), calls=%async_computation.2 | async-start | bytes 4194304 | tf_op jit(solution)/shard_map/all_to_all | solution.py:43
  152.6 2.3 gather_fusion.3
  154.9 1.3 gather_fusion.2
  156.3 0.1 select_bitcast_fusion
  156.4 0.1 copy.52
  156.5 45.6 %all-to-all-done.2 = f32[32,144,64]{1,2,0:T(8,128)S(1)} async-done(((f32[32,144,64]{1,2,0:T(8,128)}), f32[32,144,64]{1,2,0:T(8,128)S(1)}, u32[]{:S(2)}, u32[]{:S(2)}) %all-to-all-start.2) | async-done | bytes 1179680 | tf_op jit(solution)/shard_map/all_to_all | solution.py:43
  202.1 1.1 stack.5
  203.2 4.3 %all-to-all-start.4 = ((bf16[16,64,512]{2,1,0:T(8,128)(2,1)}), bf16[16,64,512]{2,1,0:T(8,128)(2,1)S(1)}, u32[]{:S(2)}, u32[]{:S(2)}) async-start(bf16[16,64,512]{2,1,0:T(8,128)(2,1)} %stack.5), calls=%async_computation.4 | async-start | bytes 2097152 | tf_op jit(solution)/shard_map/all_to_all | solution.py:70
  207.6 0.1 reduce_sum.85
  207.7 26.5 %all-to-all-done.4 = bf16[16,64,512]{2,1,0:T(8,128)(2,1)S(1)} async-done(((bf16[16,64,512]{2,1,0:T(8,128)(2,1)}), bf16[16,64,512]{2,1,0:T(8,128)(2,1)S(1)}, u32[]{:S(2)}, u32[]{:S(2)}) %all-to-all-start.4) | async-done | bytes 1048608 | tf_op jit(solution)/shard_map/all_to_all | solution.py:70
  234.2 1.2 broadcast_in_dim.20
  235.4 6.4 %all-to-all-start.3 = ((bf16[32,144,64]{1,2,0:T(8,128)(2,1)}), bf16[32,144,64]{1,2,0:T(8,128)(2,1)}, u32[]{:S(2)}, u32[]{:S(2)}) async-start(bf16[32,144,64]{1,2,0:T(8,128)(2,1)} %broadcast_in_dim.20), calls=%async_computation.3 | async-start | bytes 2097152 | tf_op jit(solution)/shard_map/all_to_all | solution.py:15
  241.9 0.3 multiply_reduce_fusion.1
  242.1 6.5 %exponential_convert_fusion = bf16[512,2048]{1,0:T(8,128)(2,1)S(1)} fusion(bf16[1024,512]{1,0:T(8,128)(2,1)S(1)} %bitcast.34, bf16[1024,2048]{1,0:T(8,128)(2,1)} %param.9, f32[512]{0:T(512)S(1)} %multiply_reduce_fusion.1, f32[2048]{0:T(1024)S(1)} %multiply_reduce_fusion), kind=kOutput, calls=%fused_computation.5 | convolution fusion | flops 2155872256 | bytes 7350272 | tf_op jit(solution)/shard_map/dot_general | solution.py:72
  248.6 22.0 %all-to-all-done.3 = bf16[32,144,64]{1,2,0:T(8,128)(2,1)} async-done(((bf16[32,144,64]{1,2,0:T(8,128)(2,1)}), bf16[32,144,64]{1,2,0:T(8,128)(2,1)}, u32[]{:S(2)}, u32[]{:S(2)}) %all-to-all-start.3) | async-done | bytes 589856 | tf_op jit(solution)/shard_map/all_to_all | solution.py:15
  270.6 2.8 fusion.16
  273.4 39.5 %all-gather.7.cloned.1.call-done = f32[2304,512]{1,0:T(8,128)} async-done(((f32[144,512]{1,0:T(8,128)}), f32[2304,512]{1,0:T(8,128)}) %all-gather.7.cloned.1.call-update) | async-done | bytes 4718608 | tf_op jit(solution)/shard_map/all_gather | solution.py:32
  312.9 2.9 reduce_sum.87
  315.8 0.1 fusion.1
  315.9 2.1 fusion.3
  318.0 0.9 reshape.48
  318.9 2.4 copy.53
  321.4 61.6 %all_to_all.30 = f32[32,144,64]{1,2,0:T(8,128)S(1)} all-to-all(f32[32,144,64]{1,2,0:T(8,128)} %copy.53), channel_id=1, replica_groups=mesh['centre'=16,'sample'=32] {'sample'}, dimensions={0} | all-to-all | bytes 2359296 | tf_op jit(solution)/shard_map/all_to_all | solution.py:43
  382.9 0.1 reduce_sum.89
  383.1 0.6 multiply_subtract_fusion
  (28 shorter events, 0.3 us)
Async XLA Ops:
  6.5 0.8 copy-start
  6.5 14.1 %copy-start.5 = (f32[144,64]{0,1:T(8,128)S(1)}, f32[144,64]{0,1:T(8,128)}, u32[]{:S(2)}) copy-start(f32[144,64]{0,1:T(8,128)} %param.13) | copy-start | bytes 110596
  13.4 33.9 %all-to-all-start = ((bf16[16,64,512]{2,1,0:T(8,128)(2,1)}), bf16[16,64,512]{2,1,0:T(8,128)(2,1)S(1)}, u32[]{:S(2)}, u32[]{:S(2)}) async-start(bf16[16,64,512]{2,1,0:T(8,128)(2,1)} %stack.4), calls=%async_computation | async-start | bytes 2097152 | tf_op jit(solution)/shard_map/all_to_all | solution.py:70
  48.4 42.3 %all-to-all-start.1 = ((bf16[32,144,64]{1,2,0:T(8,128)(2,1)}), bf16[32,144,64]{1,2,0:T(8,128)(2,1)}, u32[]{:S(2)}, u32[]{:S(2)}) async-start(bf16[32,144,64]{1,2,0:T(8,128)(2,1)} %broadcast_in_dim.19), calls=%async_computation.1 | async-start | bytes 2097152 | tf_op jit(solution)/shard_map/all_to_all | solution.py:15
  61.9 71.1 %all-gather.5.cloned.1.call-start = ((), (), s32[]{:S(2)}) async-start(), calls=%async_computation.6 | async-start | bytes 5013504 | tf_op jit(solution)/shard_map/all_gather | solution.py:32
  62.0 3.5 copy-start.1
  142.0 60.1 %all-to-all-start.2 = ((f32[32,144,64]{1,2,0:T(8,128)}), f32[32,144,64]{1,2,0:T(8,128)S(1)}, u32[]{:S(2)}, u32[]{:S(2)}) async-start(f32[32,144,64]{1,2,0:T(8,128)} %copy.47), calls=%async_computation.2 | async-start | bytes 4194304 | tf_op jit(solution)/shard_map/all_to_all | solution.py:43
  203.2 31.0 %all-to-all-start.4 = ((bf16[16,64,512]{2,1,0:T(8,128)(2,1)}), bf16[16,64,512]{2,1,0:T(8,128)(2,1)S(1)}, u32[]{:S(2)}, u32[]{:S(2)}) async-start(bf16[16,64,512]{2,1,0:T(8,128)(2,1)} %stack.5), calls=%async_computation.4 | async-start | bytes 2097152 | tf_op jit(solution)/shard_map/all_to_all | solution.py:70
  207.7 34.4 %copy-start.3 = (f32[144,64]{0,1:T(8,128)}, f32[144,64]{0,1:T(8,128)S(1)}, u32[]{:S(2)}) copy-start(f32[144,64]{0,1:T(8,128)S(1)} %reduce_sum.85) | copy-start | bytes 110596
  235.4 35.2 %all-to-all-start.3 = ((bf16[32,144,64]{1,2,0:T(8,128)(2,1)}), bf16[32,144,64]{1,2,0:T(8,128)(2,1)}, u32[]{:S(2)}, u32[]{:S(2)}) async-start(bf16[32,144,64]{1,2,0:T(8,128)(2,1)} %broadcast_in_dim.20), calls=%async_computation.3 | async-start | bytes 2097152 | tf_op jit(solution)/shard_map/all_to_all | solution.py:15
  241.8 71.1 %all-gather.7.cloned.1.call-start = ((), (), s32[]{:S(2)}) async-start(), calls=%async_computation.7 | async-start | bytes 5013504 | tf_op jit(solution)/shard_map/all_gather | solution.py:32
  248.6 64.3 %copy-start.2 = (bf16[512,2048]{1,0:T(8,128)(2,1)}, bf16[512,2048]{1,0:T(8,128)(2,1)S(1)}, u32[]{:S(2)}) copy-start(bf16[512,2048]{1,0:T(8,128)(2,1)S(1)} %exponential_convert_fusion) | copy-start | bytes 6291460
  321.4 61.7 %copy-start.4 = (f32[144,64]{0,1:T(8,128)S(1)}, f32[144,64]{0,1:T(8,128)}, u32[]{:S(2)}) copy-start(f32[144,64]{0,1:T(8,128)} %copy-done.3) | copy-start | bytes 110596
  321.4 61.7 %copy-start.6 = (f32[144,64]{0,1:T(8,128)S(1)}, f32[144,64]{0,1:T(8,128)}, u32[]{:S(2)}) copy-start(f32[144,64]{0,1:T(8,128)} %param.13) | copy-start | bytes 110596
Sparse Core Ops, SparseCore 0:
  93.6 39.3 all-gather.4
  273.5 39.3 all-gather.6
